TPU v7x, 32 devices: a whole 2x2x4 slice. The times are simulated.
32 devices in a mesh: groups: 1, chain: 4 (over y, x), tm: 8 (over z, core).
Axes of the slice: x: 2, y: 2, z: 4, core: 2. Of those that a mesh axis runs over, the one named last changes fastest.
Arguments:
- traces: bfloat16 [4, 2048, 1024], P(('groups', 'chain'), 'tm'), may hold values from -100 to 100
- lengths: int32 [4], P('groups'), may hold values from 1024 to 1793, as said below
Outputs:
- omega: float32 [1024, 1024], P(('groups', 'chain', 'tm'))
Inputs may be any that keep to these rules, and one draw needn't show every extreme that they name: `lengths`: every chain has between half of the window and 1793 valid draws; some chain has exactly each of the two ends.
All inputs are finite; a program needn't handle non-finite values.
Results may differ from a plain program's by a relative error of at most 0.0003.
Values may be sent and summed in bfloat16 or wider, within the bound.
A program may use at most 64 MiB of HBM per device.

v0:
```python
import jax
import jax.numpy as jnp
from jax import lax
from jax.sharding import PartitionSpec as P

LAG = 256


def shifted(block, axis, distance):
    devices = range(lax.axis_size(axis))
    route = [(i - distance, i) for i in devices if i - distance in devices]
    return lax.ppermute(block, axis, route)


def window_sums(current, previous):
    chains, steps, width = current.shape
    count = steps // LAG
    blocks = current.reshape(chains, count, LAG, width)
    earlier = jnp.concatenate([previous[:, None], blocks[:, :-1]], axis=1)
    index = jnp.arange(LAG)
    lower = index[None, :] <= index[:, None]
    upper = index[None, :] > index[:, None]
    lower_mat = lower.astype(jnp.float32)
    upper_mat = upper.astype(jnp.float32)
    result = jnp.einsum("ij,cbjp->cbip", lower_mat, blocks, precision=lax.Precision.HIGHEST)
    result = result + jnp.einsum(
        "ij,cbjp->cbip", upper_mat, earlier, precision=lax.Precision.HIGHEST
    )
    return result.reshape(chains, steps, width)


def gram_rows(filtered):
    chains, steps, width = filtered.shape
    flat = filtered.reshape(chains * steps, width)
    return jnp.einsum("tk,tp->kp", flat, flat, precision=lax.Precision.HIGHEST)


def on_device(traces, lengths):
    chains, steps, width = traces.shape
    own_len = lax.dynamic_slice_in_dim(lengths, lax.axis_index("chain") * chains, chains)
    first_time = lax.axis_index("tm") * steps
    times = first_time + jnp.arange(steps, dtype=jnp.int32)
    valid = (times[None, :] < own_len[:, None]).astype(jnp.float32)
    back_times = times - steps
    back_valid = ((back_times[None, :] >= 0) & (back_times[None, :] < own_len[:, None])).astype(
        jnp.float32
    )
    behind = shifted(traces, "tm", 1)
    data = traces.astype(jnp.float32) * valid[..., None]
    earlier = behind.astype(jnp.float32) * back_valid[..., None]
    totals = lax.psum(jnp.sum(data, axis=1), "tm")
    mean = totals / own_len.astype(jnp.float32)[:, None]
    scale = 1.0 / (LAG * jnp.sum(lengths).astype(jnp.float32))
    centered = window_sums(
        (data - mean[:, None, :]) * valid[..., None],
        (earlier - mean[:, None, :]) * back_valid[..., None],
    )
    return lax.psum_scatter(
        scale * gram_rows(centered), ("chain", "tm"), scatter_dimension=0, tiled=True
    )


def solution(mesh):
    in_specs = (P(("groups", "chain"), "tm", None), P("groups"))
    out_specs = P(("groups", "chain", "tm"), None)
    return jax.shard_map(
        on_device, mesh=mesh, in_specs=in_specs, out_specs=out_specs, check_vma=False
    )
```

profile of v0, /device:TPU:0, one launch (start us, length us, event | category | flops | bytes accessed | tf_op | source)
XLA Modules:
  0.0 190.3 jit_solution(5155058515386910889)
XLA Ops:
  6.5 0.0 reduce-scatter.2.cloned.1.call-start
  6.5 2.4 %collective-permute-start = (bf16[1,256,1024]{2,1,0:T(8,128)(2,1)}, bf16[1,256,1024]{2,1,0:T(8,128)(2,1)S(1)}, u32[]{:S(2)}, u32[]{:S(2)}) collective-permute-start(bf16[1,256,1024]{2,1,0:T(8,128)(2,1)} %param.2), channel_id=1, source_target_pairs={{0,1},{1,2},{2,3},{3,4},{4,5},{5,6},{6,7},{8,9},{9,10},{10,11},{11... | collective-permute-start | bytes 1572872 | tf_op jit(solution)/shard_map/ppermute | solution.py:12
  9.0 1.2 dynamic_slice.3
  10.2 0.6 compare_convert_fusion
  10.9 1.2 fusion.10
  12.1 0.7 and_convert_fusion
  13.4 1.3 reduce_sum.20
  15.4 17.0 %psum.7 = f32[1,1024]{1,0:T(1,128)S(1)} all-reduce(f32[1,1024]{1,0:T(1,128)S(1)} %bitcast.20), channel_id=1, replica_groups=mesh['groups'=1,'chain'=4,'tm'=8] {'tm'}, use_global_device_ids=true, to_apply=%region_2.0 | all-reduce | flops 1024 | bytes 8192 | tf_op jit(solution)/shard_map/psum | solution.py:51
  32.4 2.1 %fusion.2 = f32[1024,256]{1,0:T(8,128)S(1)} fusion(bf16[1,256,1024]{2,1,0:T(8,128)(2,1)} %param.2, f32[1024]{0:T(1024)S(1)} %bitcast.18, f32[256]{0:T(256)S(1)} %compare_convert_fusion), kind=kOutput, calls=%fused_computation.4 | convolution fusion | flops 806420480 | bytes 1577984 | tf_op jit(solution)/shard_map/ij,cbjp->cbip/dot_general | solution.py:25
  34.5 0.0 collective-permute-done
  34.5 1.1 fusion
  35.6 5.1 %convolution_multiply_fusion = f32[1024,1024]{1,0:T(8,128)} fusion(f32[256,1024]{0,1:T(8,128)S(1)} %fusion, f32[]{:T(128)S(6)} %div.13), kind=kOutput, calls=%fused_computation | convolution fusion | flops 3222274048 | bytes 5242884 | tf_op jit(solution)/shard_map/tk,tp->kp/dot_general | solution.py:35
  40.7 0.0 reduce-scatter.2.cloned.1.call-update
  40.7 142.8 %reduce-scatter.2.cloned.1.call-done = f32[32,1024]{1,0:T(8,128)} async-done(((f32[1024,1024]{1,0:T(8,128)}), f32[32,1024]{1,0:T(8,128)}) %reduce-scatter.2.cloned.1.call-update) | async-done | bytes 131088 | tf_op jit(solution)/shard_map/reduce_scatter | solution.py:58
  (1 shorter events, 0.0 us)
Async XLA Ops:
  6.5 176.9 %reduce-scatter.2.cloned.1.call-start = ((), (), s32[]{:S(2)}) async-start(), calls=%async_computation.1 | async-start | bytes 4325376 | tf_op jit(solution)/shard_map/reduce_scatter | solution.py:58
  6.5 28.0 %collective-permute-start = (bf16[1,256,1024]{2,1,0:T(8,128)(2,1)}, bf16[1,256,1024]{2,1,0:T(8,128)(2,1)S(1)}, u32[]{:S(2)}, u32[]{:S(2)}) collective-permute-start(bf16[1,256,1024]{2,1,0:T(8,128)(2,1)} %param.2), channel_id=1, source_target_pairs={{0,1},{1,2},{2,3},{3,4},{4,5},{5,6},{6,7},{8,9},{9,10},{10,11},{11... | collective-permute-start | bytes 1572872 | tf_op jit(solution)/shard_map/ppermute | solution.py:12
Sparse Core Ops, SparseCore 0:
  40.8 142.5 reduce-scatter.1
where the time goes:
time: 191 us; the launch traced here: 190 us
  waiting for transfers between devices  143 us (75%)
  blocking collectives  17 us (9%)
  between operations  14.8 us (8%)
  matrix products  8.29 us (4%)
  other arithmetic  3.82 us (2%)
  starting transfers between devices  2.42 us (1%)
    reduce_scatter x1, waiting for transfers between devices, on_device(): lax.psum_scatter(scale * gram_rows(centered), ('chain', 'tm'), scatter_di...  143 us
    psum x1, blocking collectives, on_device(): totals = lax.psum(jnp.sum(data, axis=1), 'tm')  17 us
    dot_general x1, matrix products, gram_rows(): return jnp.einsum('tk,tp->kp', flat, flat, precision=lax.Precision.HIGHEST)  5.08 us
  transfers between devices with their start and end apart: 2, of which 1 were waited for; matrix products, arithmetic and copies ran while one was open for 4% of the time, Pallas kernels for 0%

commit v1 on v0

--- a/solution.py
+++ b/solution.py
@@ -1,9 +1,14 @@
+import functools
+
 import jax
 import jax.numpy as jnp
 from jax import lax
+from jax.experimental import pallas as pl
+from jax.experimental.pallas import tpu as pltpu
 from jax.sharding import PartitionSpec as P
 
 LAG = 256
+MESH = pl.DeviceIdType.MESH
 
 
 def shifted(block, axis, distance):
@@ -60,9 +65,282 @@
     )
 
 
+def dot(a, b):
+    return jnp.dot(a, b, preferred_element_type=jnp.float32)
+
+
+NQ = 4
+
+
+def kernel(
+    len_ref, x_ref, o_ref, data, sums, hi, lo, hi_t, lo_t, gram, part1, part2, plane, lines,
+    done, other, s_sum, r_sum, s_x, r_x, s_halo, r_halo, s_fwd, r_fwd, s1, r1, s2, r2, s3, r3,
+    s4, r4,
+):
+    steps, width = x_ref.shape
+    half = width // 2
+    cols = half // NQ
+    rows = width // 4
+    zrows = rows // 4
+    orows = zrows // 2
+    c = lax.axis_index("chain")
+    k = lax.axis_index("tm")
+    z = k // 2
+    j = k % 2
+
+    def copy(src, dst, send, recv, **where):
+        return pltpu.make_async_remote_copy(
+            src_ref=src, dst_ref=dst, send_sem=send, recv_sem=recv, device_id=where,
+            device_id_type=MESH,
+        )
+
+    barrier = pltpu.get_barrier_semaphore()
+    for r in range(1, 8):
+        pl.semaphore_signal(barrier, inc=1, device_id={"tm": k ^ r}, device_id_type=MESH)
+    for r in (1, 2):
+        pl.semaphore_signal(barrier, inc=1, device_id={"chain": c ^ r}, device_id_type=MESH)
+
+    length = len_ref[c]
+    total_len = len_ref[0]
+    for i in range(1, len_ref.shape[0]):
+        total_len = total_len + len_ref[i]
+    scale = 1.0 / (LAG * jnp.full((1, 1), total_len, jnp.int32).astype(jnp.float32))
+
+    time = k * steps + lax.broadcasted_iota(jnp.int32, (steps, 1), 0)
+    valid = (time < length).astype(jnp.float32)
+    sums[0] = jnp.sum(x_ref[...].astype(jnp.float32) * valid, axis=0, keepdims=True)
+    own = pl.ds(pl.multiple_of(steps + steps * j, steps), steps)
+    data[own, :] = x_ref[...]
+
+    @pl.when(z == 0)
+    def _():
+        data[0:steps, :] = jnp.zeros((steps, width), data.dtype)
+
+    pl.semaphore_wait(barrier, 9)
+
+    sum_copies = [
+        copy(sums.at[0], sums.at[r], s_sum.at[r], r_sum.at[r], tm=k ^ r) for r in range(1, 8)
+    ]
+    for cp in sum_copies:
+        cp.start()
+    halo_copies = [
+        copy(
+            x_ref.at[:, pl.ds(half * h, half)],
+            data.at[pl.ds(0, steps), pl.ds(half * h, half)],
+            s_halo.at[h], r_halo, tm=2 * jnp.minimum(z + 1, 3) + h,
+        )
+        for h in range(2)
+    ]
+
+    @pl.when((j == 1) & (z < 3))
+    def _():
+        for cp in halo_copies:
+            cp.start()
+
+    x_copy = copy(x_ref, data.at[own, :], s_x, r_x, tm=k ^ 1)
+    x_copy.start()
+
+    i_idx = lax.broadcasted_iota(jnp.int32, (steps, 2 * steps), 0)
+    r_idx = lax.broadcasted_iota(jnp.int32, (steps, 2 * steps), 1)
+    for cp in sum_copies:
+        cp.wait_recv()
+    total = sums[0]
+    for r in range(1, 8):
+        total = total + sums[r]
+    mean = total / jnp.full((1, 1), length, jnp.int32).astype(jnp.float32)
+
+    def windows(b):
+        first = 2 * steps * z + steps * b
+        when = first - steps + r_idx
+        keep = (r_idx > i_idx) & (r_idx <= i_idx + LAG) & (when >= 0) & (when < length)
+        band = keep.astype(jnp.float32).astype(jnp.bfloat16)
+        t = first + lax.broadcasted_iota(jnp.int32, (steps, 1), 0)
+        count = jnp.maximum(
+            jnp.minimum(t + 1, length) - jnp.maximum(t - (LAG - 1), 0), 0
+        ).astype(jnp.float32)
+        out = slice(steps * b, steps * (b + 1))
+        for n in range(width // 256):
+            at = slice(256 * n, 256 * (n + 1))
+            w = dot(band, data[steps * b : steps * (b + 2), at]) - count * mean[:, at]
+            h = w.astype(jnp.bfloat16)
+            e = (w - h.astype(jnp.float32)).astype(jnp.bfloat16)
+            hi[out, at] = h
+            lo[out, at] = e
+            hi_t[at, out] = h.T
+            lo_t[at, out] = e.T
+
+    x_copy.wait_recv()
+    windows(1)
+    mine = pl.ds(pl.multiple_of(half * j, half), half)
+    forward = copy(
+        data.at[pl.ds(0, steps), mine], data.at[pl.ds(0, steps), mine], s_fwd, r_fwd, tm=k ^ 1
+    )
+
+    @pl.when(z > 0)
+    def _():
+        copy(
+            x_ref.at[:, pl.ds(0, half)], data.at[pl.ds(0, steps), mine], s_halo.at[0], r_halo,
+            tm=k ^ 1,
+        ).wait_recv()
+        forward.start()
+        forward.wait_recv()
+
+    windows(0)
+
+    first_hop, second_hop, z_hops, swaps = [], [], [], []
+    for q in range(NQ):
+        m1 = 1 + q % 2
+        m2 = 3 - m1
+        first_hop.append([
+            copy(gram.at[q, m1], part1.at[q, 0], s1.at[q, 0], r1.at[q, 0], chain=c ^ m1),
+            copy(gram.at[q, 3], part1.at[q, 1], s1.at[q, 1], r1.at[q, 1], chain=c ^ m1),
+        ])
+        second_hop.append(copy(gram.at[q, m2], part2.at[q], s2.at[q], r2.at[q], chain=c ^ m2))
+        z_hops.append([
+            copy(
+                plane.at[q, pl.ds(pl.multiple_of(zrows * (z ^ s), zrows), zrows), :],
+                lines.at[q, s - 1], s3.at[q, s - 1], r3.at[q, s - 1], tm=k ^ (2 * s),
+            )
+            for s in range(1, 4)
+        ])
+        swaps.append(
+            copy(
+                done.at[q, pl.ds(pl.multiple_of(orows * (1 - j), orows), orows), :],
+                other.at[q], s4.at[q], r4.at[q], tm=k ^ 1,
+            )
+        )
+
+    def hop2(q):
+        m2 = 2 - q % 2
+        first_hop[q][1].wait_recv()
+        gram[q, m2] = gram[q, m2] + part1[q, 1]
+        second_hop[q].start()
+
+    def hop3(q):
+        first_hop[q][0].wait_recv()
+        second_hop[q].wait_recv()
+        plane[q] = gram[q, 0] + part1[q, 0] + part2[q]
+        for cp in z_hops[q]:
+            cp.start()
+
+    def hop4(q):
+        here = plane[q, pl.ds(pl.multiple_of(zrows * z, zrows), zrows), :]
+        for s in range(3):
+            z_hops[q][s].wait_recv()
+            here = here + lines[q, s]
+        done[q] = here * scale
+        swaps[q].start()
+
+    for p in range(NQ // 2):
+        at = pl.ds(pl.multiple_of(half * j + 2 * cols * p, 2 * cols), 2 * cols)
+        right_hi = hi[:, at]
+        right_lo = lo[:, at]
+        for r in (3, 1, 2, 0):
+            left = pl.ds(pl.multiple_of(rows * (c ^ r), rows), rows)
+            g = (
+                dot(hi_t[left, :], right_lo)
+                + dot(lo_t[left, :], right_hi)
+                + dot(hi_t[left, :], right_hi)
+            )
+            for b in range(2):
+                gram[2 * p + b, r] = g[:, cols * b : cols * (b + 1)]
+            if r == 3:
+                first_hop[2 * p][1].start()
+                first_hop[2 * p + 1][1].start()
+            elif r:
+                first_hop[2 * p + r - 1][0].start()
+
+    for q in range(NQ):
+        hop2(q)
+    for q in range(NQ):
+        hop3(q)
+    for q in range(NQ):
+        hop4(q)
+    for q in range(NQ):
+        o_ref[:, pl.ds(pl.multiple_of(half * j + cols * q, cols), cols)] = done[
+            q, pl.ds(pl.multiple_of(orows * j, orows), orows), :
+        ]
+        swaps[q].wait_recv()
+        o_ref[:, pl.ds(pl.multiple_of(half * (1 - j) + cols * q, cols), cols)] = other[q]
+
+    for cp in sum_copies:
+        cp.wait_send()
+    x_copy.wait_send()
+
+    @pl.when((j == 1) & (z < 3))
+    def _():
+        for cp in halo_copies:
+            cp.wait_send()
+
+    @pl.when(z > 0)
+    def _():
+        forward.wait_send()
+
+    for q in range(NQ):
+        for cp in first_hop[q]:
+            cp.wait_send()
+        second_hop[q].wait_send()
+        for cp in z_hops[q]:
+            cp.wait_send()
+        swaps[q].wait_send()
+
+
+def fused(traces, lengths):
+    _, steps, width = traces.shape
+    f32, bf16 = jnp.float32, jnp.bfloat16
+    rows, cols = width // 4, width // 2 // NQ
+    dma = pltpu.SemaphoreType.DMA
+    return pl.pallas_call(
+        kernel,
+        out_shape=jax.ShapeDtypeStruct((width // 32, width), f32),
+        in_specs=[
+            pl.BlockSpec(memory_space=pltpu.SMEM),
+            pl.BlockSpec(memory_space=pltpu.VMEM),
+        ],
+        out_specs=pl.BlockSpec(memory_space=pltpu.VMEM),
+        scratch_shapes=[
+            pltpu.VMEM((3 * steps, width), bf16),
+            pltpu.VMEM((8, 1, width), f32),
+            pltpu.VMEM((2 * steps, width), bf16),
+            pltpu.VMEM((2 * steps, width), bf16),
+            pltpu.VMEM((width, 2 * steps), bf16),
+            pltpu.VMEM((width, 2 * steps), bf16),
+            pltpu.VMEM((NQ, 4, rows, cols), f32),
+            pltpu.VMEM((NQ, 2, rows, cols), f32),
+            pltpu.VMEM((NQ, rows, cols), f32),
+            pltpu.VMEM((NQ, rows, cols), f32),
+            pltpu.VMEM((NQ, 3, rows // 4, cols), f32),
+            pltpu.VMEM((NQ, rows // 4, cols), f32),
+            pltpu.VMEM((NQ, rows // 8, cols), f32),
+            dma((8,)), dma((8,)),
+            dma, dma,
+            dma((2,)), dma,
+            dma, dma,
+            dma((NQ, 2)), dma((NQ, 2)),
+            dma((NQ,)), dma((NQ,)),
+            dma((NQ, 3)), dma((NQ, 3)),
+            dma((NQ,)), dma((NQ,)),
+        ],
+        compiler_params=pltpu.CompilerParams(
+            collective_id=0, has_side_effects=True, vmem_limit_bytes=48 * 1024 * 1024
+        ),
+    )(lengths, traces.reshape(steps, width))
+
+
+def body(mesh, traces, lengths):
+    chains, steps, width = traces.shape
+    laid_out = (
+        mesh.shape["groups"] == 1 and mesh.shape["chain"] == 4 and mesh.shape["tm"] == 8
+    )
+    if laid_out and chains == 1 and steps == LAG and width % 1024 == 0:
+        return fused(traces, lengths)
+    return on_device(traces, lengths)
+
+
 def solution(mesh):
     in_specs = (P(("groups", "chain"), "tm", None), P("groups"))
     out_specs = P(("groups", "chain", "tm"), None)
     return jax.shard_map(
-        on_device, mesh=mesh, in_specs=in_specs, out_specs=out_specs, check_vma=False
-    )
+        functools.partial(body, mesh), mesh=mesh, in_specs=in_specs, out_specs=out_specs,
+        check_vma=False,
+    )

time: 191 us -> 46.6 us (0.24)
  waiting for transfers between devices: 143 us -> 0 us
  Pallas kernels: 0 us -> 44 us
  blocking collectives: 17 us -> 0 us
  between operations: 14.8 us -> 0.01 us
  matrix products: 8.29 us -> 0 us
  other arithmetic: 3.82 us -> 0 us
  starting transfers between devices: 2.42 us -> 0 us
    reduce_scatter x1 -> x0, waiting for transfers between devices: 143 us -> none  [on_device(): lax.psum_scatter(scale * gram_rows(centered), ('chain', 'tm'), scatter_di...]
    pallas_call x0 -> x1, Pallas kernels: none -> 44 us  [fused(): pl.pallas_call(kernel, out_shape=jax.ShapeDtypeStruct((width // 32, width...]
    psum x1 -> x0, blocking collectives: 17 us -> none  [on_device(): totals = lax.psum(jnp.sum(data, axis=1), 'tm')]
    dot_general x3 -> x0, matrix products: 8.29 us -> none  [the longest x1 5.08 us: gram_rows(): return jnp.einsum('tk,tp->kp', flat, flat, precision=lax.Precision.HIGHEST)]
    reduce_sum x2 -> x0, other arithmetic: 2.51 us -> none  [the longest x1 1.29 us: on_device(): scale = 1.0 / (LAG * jnp.sum(lengths).astype(jnp.float32))]
    ppermute x1 -> x0, starting transfers between devices: 2.42 us -> none  [shifted(): return lax.ppermute(block, axis, route)]
    unnamed x0 -> x5, local copies, waits for them, and re-layouts: none -> 2.35 us
  transfers between devices with their start and end apart: 2 -> 0, of which waited for: 1 -> 0; matrix products, arithmetic and copies ran while one was open for 4% -> 0% of each run, Pallas kernels for 0% -> 0%
where the time goes in v1:
time: 46.6 us; the launch traced here: 46.4 us
  Pallas kernels  44 us (94%)
  local copies, waits for them, and re-layouts  2.35 us (5%)
    pallas_call x1, Pallas kernels, fused(): pl.pallas_call(kernel, out_shape=jax.ShapeDtypeStruct((width // 32, width...  44 us
    unnamed x5, local copies, waits for them, and re-layouts  2.35 us

profile of v1, /device:TPU:0, one launch (start us, length us, event | category | flops | bytes accessed | tf_op | source)
XLA Modules:
  0.0 46.4 jit_solution(16599165375052958002)
XLA Ops:
  0.0 0.0 copy-start.1
  0.0 0.7 %copy-done.1 = s32[4]{0:T(128)S(1)} copy-done((s32[4]{0:T(128)S(1)}, s32[4]{0:T(128)}, u32[]{:S(2)}) %copy-start.1) | copy-done | bytes 40
  0.7 0.0 copy-start
  0.7 1.0 %copy-done = bf16[1,256,1024]{2,1,0:T(8,128)(2,1)S(1)} copy-done((bf16[1,256,1024]{2,1,0:T(8,128)(2,1)S(1)}, bf16[1,256,1024]{2,1,0:T(8,128)(2,1)}, u32[]{:S(2)}) %copy-start) | copy-done | bytes 524312
  1.7 44.0 %shard_map.28 = f32[32,1024]{1,0:T(8,128)S(1)} custom-call(s32[4]{0:T(128)S(1)} %copy-done.1, bf16[256,1024]{1,0:T(8,128)(2,1)S(1)} %bitcast.1), custom_call_target="tpu_custom_call" | custom-call | tf_op jit(solution)/shard_map/pallas_call | solution.py:293
  45.7 0.7 %copy.4 = f32[32,1024]{1,0:T(8,128)} copy(f32[32,1024]{1,0:T(8,128)S(1)} %shard_map.28) | data formatting | bytes 262144
Async XLA Ops:
  0.0 0.7 %copy-start.1 = (s32[4]{0:T(128)S(1)}, s32[4]{0:T(128)}, u32[]{:S(2)}) copy-start(s32[4]{0:T(128)} %len_ref.1) | copy-start | bytes 52
  0.7 1.0 %copy-start = (bf16[1,256,1024]{2,1,0:T(8,128)(2,1)S(1)}, bf16[1,256,1024]{2,1,0:T(8,128)(2,1)}, u32[]{:S(2)}) copy-start(bf16[1,256,1024]{2,1,0:T(8,128)(2,1)} %param.2) | copy-start | bytes 1572868

commit v2 on v1

--- a/solution.py
+++ b/solution.py
@@ -70,12 +70,13 @@
 
 
 NQ = 4
+TOP = 32767.0
 
 
 def kernel(
-    len_ref, x_ref, o_ref, data, sums, hi, lo, hi_t, lo_t, gram, part1, part2, plane, lines,
-    done, other, s_sum, r_sum, s_x, r_x, s_halo, r_halo, s_fwd, r_fwd, s1, r1, s2, r2, s3, r3,
-    s4, r4,
+    len_ref, x_ref, o_ref, data, sums, hi, lo, hi_t, lo_t, keep, code1, scale1, got1,
+    gots1, code2, scale2, got2, gots2, plane, code3, scale3, got3, gots3, done, other, s_sum, r_sum, s_x, r_x, s_halo, r_halo, s_fwd, r_fwd, s1, r1, s1s,
+    r1s, s2, r2, s2s, r2s, s3, r3, s3s, r3s, s4, r4,
 ):
     steps, width = x_ref.shape
     half = width // 2
@@ -187,19 +188,57 @@
 
     windows(0)
 
+    def send(codes, scales, to_codes, to_scales, sems, at, **where):
+        (sc, rc), (ss, rs) = sems
+        return [
+            copy(codes, to_codes, sc.at[at], rc.at[at], **where),
+            copy(scales, to_scales, ss.at[at], rs.at[at], **where),
+        ]
+
+    def start(copies):
+        for cp in copies:
+            cp.start()
+
+    def arrive(copies):
+        for cp in copies:
+            cp.wait_recv()
+
+    def pack(values, codes, scales, at):
+        for g in range(8):
+            v = values(g)
+            top = jnp.maximum(jnp.max(jnp.abs(v), axis=0, keepdims=True), 1e-33)
+            scales[(*at, g // 2, slice(g % 2, g % 2 + 1))] = top * (1.0 / TOP)
+            code = jnp.round(v * (TOP / top)).astype(jnp.int32).astype(jnp.int16)
+            codes[(*at, slice(32 * g, 32 * g + 32))] = code
+
+    def unpack(codes, scales, at, g, base=None):
+        code = codes[(*at, slice(32 * g, 32 * g + 32))].astype(jnp.int32).astype(jnp.float32)
+        if base is None:
+            return code * scales[(*at, g // 2, slice(g % 2, g % 2 + 1))]
+        return code * scales[(*at, slice(g, g + 1))]
+
     first_hop, second_hop, z_hops, swaps = [], [], [], []
     for q in range(NQ):
         m1 = 1 + q % 2
         m2 = 3 - m1
         first_hop.append([
-            copy(gram.at[q, m1], part1.at[q, 0], s1.at[q, 0], r1.at[q, 0], chain=c ^ m1),
-            copy(gram.at[q, 3], part1.at[q, 1], s1.at[q, 1], r1.at[q, 1], chain=c ^ m1),
+            send(
+                code1.at[q, i], scale1.at[q, i], got1.at[q, i], gots1.at[q, i],
+                ((s1, r1), (s1s, r1s)), (q, i), chain=c ^ m1,
+            )
+            for i in range(2)
         ])
-        second_hop.append(copy(gram.at[q, m2], part2.at[q], s2.at[q], r2.at[q], chain=c ^ m2))
+        second_hop.append(
+            send(
+                code2.at[q], scale2.at[q], got2.at[q], gots2.at[q], ((s2, r2), (s2s, r2s)), q,
+                chain=c ^ m2,
+            )
+        )
         z_hops.append([
-            copy(
-                plane.at[q, pl.ds(pl.multiple_of(zrows * (z ^ s), zrows), zrows), :],
-                lines.at[q, s - 1], s3.at[q, s - 1], r3.at[q, s - 1], tm=k ^ (2 * s),
+            send(
+                code3.at[q, pl.ds(pl.multiple_of(zrows * (z ^ s), zrows), zrows), :],
+                scale3.at[q, z ^ s], got3.at[q, s - 1], gots3.at[q, s - 1],
+                ((s3, r3), (s3s, r3s)), (q, s - 1), tm=k ^ (2 * s),
             )
             for s in range(1, 4)
         ])
@@ -211,49 +250,76 @@
         )
 
     def hop2(q):
-        m2 = 2 - q % 2
-        first_hop[q][1].wait_recv()
-        gram[q, m2] = gram[q, m2] + part1[q, 1]
-        second_hop[q].start()
+        arrive(first_hop[q][1])
+        pack(
+            lambda g: keep[q, 1, 32 * g : 32 * g + 32] + unpack(got1, gots1, (q, 1), g),
+            code2, scale2, (q,),
+        )
+        start(second_hop[q])
 
     def hop3(q):
-        first_hop[q][0].wait_recv()
-        second_hop[q].wait_recv()
-        plane[q] = gram[q, 0] + part1[q, 0] + part2[q]
-        for cp in z_hops[q]:
-            cp.start()
+        arrive(first_hop[q][0])
+        arrive(second_hop[q])
+
+        def value(g):
+            v = (
+                keep[q, 0, 32 * g : 32 * g + 32]
+                + unpack(got1, gots1, (q, 0), g)
+                + unpack(got2, gots2, (q,), g)
+            )
+            plane[q, 32 * g : 32 * g + 32] = v
+            return v
+
+        pack(value, code3, scale3, (q,))
+        for copies in z_hops[q]:
+            start(copies)
 
     def hop4(q):
-        here = plane[q, pl.ds(pl.multiple_of(zrows * z, zrows), zrows), :]
         for s in range(3):
-            z_hops[q][s].wait_recv()
-            here = here + lines[q, s]
-        done[q] = here * scale
+            arrive(z_hops[q][s])
+        for g in range(2):
+            at = pl.ds(pl.multiple_of(zrows * z + orows * g, orows), orows)
+            here = plane[q, at, :]
+            for s in range(3):
+                here = here + unpack(got3, gots3, (q, s), g, 0)
+            done[q, 32 * g : 32 * g + 32] = here * scale
         swaps[q].start()
 
-    for p in range(NQ // 2):
+    def products(p, go):
         at = pl.ds(pl.multiple_of(half * j + 2 * cols * p, 2 * cols), 2 * cols)
         right_hi = hi[:, at]
         right_lo = lo[:, at]
         for r in (3, 1, 2, 0):
             left = pl.ds(pl.multiple_of(rows * (c ^ r), rows), rows)
-            g = (
+            w = (
                 dot(hi_t[left, :], right_lo)
                 + dot(lo_t[left, :], right_hi)
                 + dot(hi_t[left, :], right_hi)
             )
             for b in range(2):
-                gram[2 * p + b, r] = g[:, cols * b : cols * (b + 1)]
-            if r == 3:
-                first_hop[2 * p][1].start()
-                first_hop[2 * p + 1][1].start()
-            elif r:
-                first_hop[2 * p + r - 1][0].start()
-
-    for q in range(NQ):
-        hop2(q)
-    for q in range(NQ):
-        hop3(q)
+                q = 2 * p + b
+                part = w[:, cols * b : cols * (b + 1)]
+                if r == 3 or r == 1 + b:
+                    slot = int(r == 3)
+                    pack(lambda g: part[32 * g : 32 * g + 32], code1, scale1, (q, slot))
+                    if go:
+                        start(first_hop[q][slot])
+                else:
+                    keep[q, int(r != 0)] = part
+
+    products(0, True)
+    products(1, False)
+    hop2(0)
+    hop2(1)
+    for i in (1, 0):
+        start(first_hop[2][i])
+        start(first_hop[3][i])
+    hop3(0)
+    hop3(1)
+    hop2(2)
+    hop2(3)
+    hop3(2)
+    hop3(3)
     for q in range(NQ):
         hop4(q)
     for q in range(NQ):
@@ -277,17 +343,15 @@
         forward.wait_send()
 
     for q in range(NQ):
-        for cp in first_hop[q]:
-            cp.wait_send()
-        second_hop[q].wait_send()
-        for cp in z_hops[q]:
-            cp.wait_send()
+        for copies in (*first_hop[q], second_hop[q], *z_hops[q]):
+            for cp in copies:
+                cp.wait_send()
         swaps[q].wait_send()
 
 
 def fused(traces, lengths):
     _, steps, width = traces.shape
-    f32, bf16 = jnp.float32, jnp.bfloat16
+    f32, bf16, i16 = jnp.float32, jnp.bfloat16, jnp.int16
     rows, cols = width // 4, width // 2 // NQ
     dma = pltpu.SemaphoreType.DMA
     return pl.pallas_call(
@@ -305,20 +369,29 @@
             pltpu.VMEM((2 * steps, width), bf16),
             pltpu.VMEM((width, 2 * steps), bf16),
             pltpu.VMEM((width, 2 * steps), bf16),
-            pltpu.VMEM((NQ, 4, rows, cols), f32),
             pltpu.VMEM((NQ, 2, rows, cols), f32),
+            pltpu.VMEM((NQ, 2, rows, cols), i16),
+            pltpu.VMEM((NQ, 2, 4, 2, cols), f32),
+            pltpu.VMEM((NQ, 2, rows, cols), i16),
+            pltpu.VMEM((NQ, 2, 4, 2, cols), f32),
+            pltpu.VMEM((NQ, rows, cols), i16),
+            pltpu.VMEM((NQ, 4, 2, cols), f32),
+            pltpu.VMEM((NQ, rows, cols), i16),
+            pltpu.VMEM((NQ, 4, 2, cols), f32),
             pltpu.VMEM((NQ, rows, cols), f32),
-            pltpu.VMEM((NQ, rows, cols), f32),
-            pltpu.VMEM((NQ, 3, rows // 4, cols), f32),
+            pltpu.VMEM((NQ, rows, cols), i16),
+            pltpu.VMEM((NQ, 4, 2, cols), f32),
+            pltpu.VMEM((NQ, 3, rows // 4, cols), i16),
+            pltpu.VMEM((NQ, 3, 2, cols), f32),
             pltpu.VMEM((NQ, rows // 4, cols), f32),
             pltpu.VMEM((NQ, rows // 8, cols), f32),
             dma((8,)), dma((8,)),
             dma, dma,
             dma((2,)), dma,
             dma, dma,
-            dma((NQ, 2)), dma((NQ, 2)),
-            dma((NQ,)), dma((NQ,)),
-            dma((NQ, 3)), dma((NQ, 3)),
+            dma((NQ, 2)), dma((NQ, 2)), dma((NQ, 2)), dma((NQ, 2)),
+            dma((NQ,)), dma((NQ,)), dma((NQ,)), dma((NQ,)),
+            dma((NQ, 3)), dma((NQ, 3)), dma((NQ, 3)), dma((NQ, 3)),
             dma((NQ,)), dma((NQ,)),
         ],
         compiler_params=pltpu.CompilerParams(
@@ -332,7 +405,7 @@
     laid_out = (
         mesh.shape["groups"] == 1 and mesh.shape["chain"] == 4 and mesh.shape["tm"] == 8
     )
-    if laid_out and chains == 1 and steps == LAG and width % 1024 == 0:
+    if laid_out and chains == 1 and steps == LAG and width == 1024:
         return fused(traces, lengths)
     return on_device(traces, lengths)
 

time: 46.6 us -> 36.8 us (0.79)
  Pallas kernels: 44 us -> 34.3 us
    pallas_call x1, Pallas kernels: 44 us -> 34.3 us  [fused(): pl.pallas_call(kernel, out_shape=jax.ShapeDtypeStruct((width // 32, width...]
where the time goes in v2:
time: 36.8 us; the launch traced here: 36.7 us
  Pallas kernels  34.3 us (93%)
  local copies, waits for them, and re-layouts  2.35 us (6%)
    pallas_call x1, Pallas kernels, fused(): pl.pallas_call(kernel, out_shape=jax.ShapeDtypeStruct((width // 32, width...  34.3 us
    unnamed x5, local copies, waits for them, and re-layouts  2.35 us

profile of v2, /device:TPU:0, one launch (start us, length us, event | category | flops | bytes accessed | tf_op | source)
XLA Modules:
  0.0 36.7 jit_solution(4806748101892492518)
XLA Ops:
  0.0 0.0 copy-start.1
  0.0 0.7 %copy-done.1 = s32[4]{0:T(128)S(1)} copy-done((s32[4]{0:T(128)S(1)}, s32[4]{0:T(128)}, u32[]{:S(2)}) %copy-start.1) | copy-done | bytes 40
  0.7 0.0 copy-start
  0.7 1.0 %copy-done = bf16[1,256,1024]{2,1,0:T(8,128)(2,1)S(1)} copy-done((bf16[1,256,1024]{2,1,0:T(8,128)(2,1)S(1)}, bf16[1,256,1024]{2,1,0:T(8,128)(2,1)}, u32[]{:S(2)}) %copy-start) | copy-done | bytes 524312
  1.7 34.3 %shard_map.28 = f32[32,1024]{1,0:T(8,128)S(1)} custom-call(s32[4]{0:T(128)S(1)} %copy-done.1, bf16[256,1024]{1,0:T(8,128)(2,1)S(1)} %bitcast.1), custom_call_target="tpu_custom_call" | custom-call | tf_op jit(solution)/shard_map/pallas_call | solution.py:357
  36.0 0.7 %copy.4 = f32[32,1024]{1,0:T(8,128)} copy(f32[32,1024]{1,0:T(8,128)S(1)} %shard_map.28) | data formatting | bytes 262144
Async XLA Ops:
  0.0 0.7 %copy-start.1 = (s32[4]{0:T(128)S(1)}, s32[4]{0:T(128)}, u32[]{:S(2)}) copy-start(s32[4]{0:T(128)} %len_ref.1) | copy-start | bytes 52
  0.7 1.0 %copy-start = (bf16[1,256,1024]{2,1,0:T(8,128)(2,1)S(1)}, bf16[1,256,1024]{2,1,0:T(8,128)(2,1)}, u32[]{:S(2)}) copy-start(bf16[1,256,1024]{2,1,0:T(8,128)(2,1)} %param.2) | copy-start | bytes 1572868

commit v3 on v2

--- a/solution.py
+++ b/solution.py
@@ -74,11 +74,13 @@
 
 
 def kernel(
-    len_ref, x_ref, o_ref, data, sums, hi, lo, hi_t, lo_t, keep, code1, scale1, got1,
-    gots1, code2, scale2, got2, gots2, plane, code3, scale3, got3, gots3, done, other, s_sum, r_sum, s_x, r_x, s_halo, r_halo, s_fwd, r_fwd, s1, r1, s1s,
+    len_hbm, x_hbm, o_ref, len_ref, data, ext, hi_e, lo_e, hi_et, lo_et, sums, hi, lo, hi_t, lo_t, keep, code1, scale1, got1,
+    gots1, code2, scale2, got2, gots2, plane, code3, scale3, got3, gots3, done, other, in_sem, s_sum, r_sum, s_x, r_x,
+    s_halo, r_halo, s_fwd, r_fwd, s1, r1, s1s,
     r1s, s2, r2, s2s, r2s, s3, r3, s3s, r3s, s4, r4,
 ):
-    steps, width = x_ref.shape
+    steps, width = x_hbm.shape
+    pad = steps // 2
     half = width // 2
     cols = half // NQ
     rows = width // 4
@@ -95,12 +97,26 @@
             device_id_type=MESH,
         )
 
+    def start(copies):
+        for cp in copies:
+            cp.start()
+
+    def arrive(copies):
+        for cp in copies:
+            cp.wait_recv()
+
+    own = pl.ds(pl.multiple_of(pad + steps * j, pad), steps)
+    len_in = pltpu.make_async_copy(len_hbm, len_ref, in_sem.at[0])
+    x_in = pltpu.make_async_copy(x_hbm, data.at[own, :], in_sem.at[1])
+    len_in.start()
+    x_in.start()
     barrier = pltpu.get_barrier_semaphore()
     for r in range(1, 8):
         pl.semaphore_signal(barrier, inc=1, device_id={"tm": k ^ r}, device_id_type=MESH)
     for r in (1, 2):
         pl.semaphore_signal(barrier, inc=1, device_id={"chain": c ^ r}, device_id_type=MESH)
 
+    len_in.wait()
     length = len_ref[c]
     total_len = len_ref[0]
     for i in range(1, len_ref.shape[0]):
@@ -109,13 +125,16 @@
 
     time = k * steps + lax.broadcasted_iota(jnp.int32, (steps, 1), 0)
     valid = (time < length).astype(jnp.float32)
-    sums[0] = jnp.sum(x_ref[...].astype(jnp.float32) * valid, axis=0, keepdims=True)
-    own = pl.ds(pl.multiple_of(steps + steps * j, steps), steps)
-    data[own, :] = x_ref[...]
+    x_in.wait()
+    sums[0] = jnp.sum(data[own, :].astype(jnp.float32) * valid, axis=0, keepdims=True)
 
     @pl.when(z == 0)
     def _():
-        data[0:steps, :] = jnp.zeros((steps, width), data.dtype)
+        data[0:pad, :] = jnp.zeros((pad, width), data.dtype)
+
+    @pl.when(z == 3)
+    def _():
+        data[5 * pad : 6 * pad, :] = jnp.zeros((pad, width), data.dtype)
 
     pl.semaphore_wait(barrier, 9)
 
@@ -124,22 +143,46 @@
     ]
     for cp in sum_copies:
         cp.start()
-    halo_copies = [
-        copy(
-            x_ref.at[:, pl.ds(half * h, half)],
-            data.at[pl.ds(0, steps), pl.ds(half * h, half)],
-            s_halo.at[h], r_halo, tm=2 * jnp.minimum(z + 1, 3) + h,
+    def halo(way, h):
+        near = 2 * jnp.minimum(z + 1, 3) if way == 0 else 2 * jnp.maximum(z - 1, 0)
+        take = 4 * pad if way == 0 else pad
+        put = 0 if way == 0 else 5 * pad
+        at = pl.ds(half * h, half)
+        return copy(
+            data.at[pl.ds(take, pad), at], data.at[pl.ds(put, pad), at], s_halo.at[h],
+            r_halo.at[way], tm=near + h,
         )
-        for h in range(2)
-    ]
+
+    ups = [halo(0, h) for h in range(2)]
+    downs = [halo(1, h) for h in range(2)]
 
     @pl.when((j == 1) & (z < 3))
     def _():
-        for cp in halo_copies:
-            cp.start()
-
-    x_copy = copy(x_ref, data.at[own, :], s_x, r_x, tm=k ^ 1)
+        start(ups)
+
+    @pl.when((j == 0) & (z > 0))
+    def _():
+        start(downs)
+
+    x_copy = copy(data.at[own, :], data.at[own, :], s_x, r_x, tm=k ^ 1)
     x_copy.start()
+
+    mine = pl.ds(pl.multiple_of(half * j, half), half)
+    forwards, landed = [], []
+    for way, put in ((0, 0), (1, 5 * pad)):
+        block = data.at[pl.ds(put, pad), mine]
+        forwards.append(copy(block, block, s_fwd.at[way], r_fwd.at[way], tm=k ^ 1))
+        landed.append(copy(block, block, s_halo.at[0], r_halo.at[way], tm=k ^ 1))
+
+    @pl.when(z > 0)
+    def _():
+        landed[0].wait_recv()
+        forwards[0].start()
+
+    @pl.when(z < 3)
+    def _():
+        landed[1].wait_recv()
+        forwards[1].start()
 
     i_idx = lax.broadcasted_iota(jnp.int32, (steps, 2 * steps), 0)
     r_idx = lax.broadcasted_iota(jnp.int32, (steps, 2 * steps), 1)
@@ -151,7 +194,7 @@
     mean = total / jnp.full((1, 1), length, jnp.int32).astype(jnp.float32)
 
     def windows(b):
-        first = 2 * steps * z + steps * b
+        first = 2 * steps * z + pad + steps * b
         when = first - steps + r_idx
         keep = (r_idx > i_idx) & (r_idx <= i_idx + LAG) & (when >= 0) & (when < length)
         band = keep.astype(jnp.float32).astype(jnp.bfloat16)
@@ -171,22 +214,48 @@
             lo_t[at, out] = e.T
 
     x_copy.wait_recv()
+
+    @pl.when(z == 0)
+    def _():
+        row = lax.broadcasted_iota(jnp.int32, (pad, pad), 0)
+        col = lax.broadcasted_iota(jnp.int32, (pad, pad), 1)
+        band = ((col <= row) & (col < length)).astype(jnp.float32).astype(jnp.bfloat16)
+        t = lax.broadcasted_iota(jnp.int32, (pad, 1), 0)
+        count = jnp.minimum(t + 1, length).astype(jnp.float32)
+        for n in range(width // 256):
+            at = slice(256 * n, 256 * (n + 1))
+            w = dot(band, data[pad : 2 * pad, at]) - count * mean[:, at]
+            h = w.astype(jnp.bfloat16)
+            e = (w - h.astype(jnp.float32)).astype(jnp.bfloat16)
+            hi_e[:, at] = h
+            lo_e[:, at] = e
+            hi_et[at, :] = h.T
+            lo_et[at, :] = e.T
+        for p in range(NQ // 2):
+            at = pl.ds(pl.multiple_of(half * j + 2 * cols * p, 2 * cols), 2 * cols)
+            for r in range(4):
+                left = pl.ds(pl.multiple_of(rows * (c ^ r), rows), rows)
+                ext[p, r] = (
+                    dot(hi_et[left, :], lo_e[:, at])
+                    + dot(lo_et[left, :], hi_e[:, at])
+                    + dot(hi_et[left, :], hi_e[:, at])
+                )
+
+    @pl.when(z != 0)
+    def _():
+        ext[...] = jnp.zeros_like(ext)
+
+    @pl.when(z > 0)
+    def _():
+        forwards[0].wait_recv()
+
+    windows(0)
+
+    @pl.when(z < 3)
+    def _():
+        forwards[1].wait_recv()
+
     windows(1)
-    mine = pl.ds(pl.multiple_of(half * j, half), half)
-    forward = copy(
-        data.at[pl.ds(0, steps), mine], data.at[pl.ds(0, steps), mine], s_fwd, r_fwd, tm=k ^ 1
-    )
-
-    @pl.when(z > 0)
-    def _():
-        copy(
-            x_ref.at[:, pl.ds(0, half)], data.at[pl.ds(0, steps), mine], s_halo.at[0], r_halo,
-            tm=k ^ 1,
-        ).wait_recv()
-        forward.start()
-        forward.wait_recv()
-
-    windows(0)
 
     def send(codes, scales, to_codes, to_scales, sems, at, **where):
         (sc, rc), (ss, rs) = sems
@@ -194,14 +263,6 @@
             copy(codes, to_codes, sc.at[at], rc.at[at], **where),
             copy(scales, to_scales, ss.at[at], rs.at[at], **where),
         ]
-
-    def start(copies):
-        for cp in copies:
-            cp.start()
-
-    def arrive(copies):
-        for cp in copies:
-            cp.wait_recv()
 
     def pack(values, codes, scales, at):
         for g in range(8):
@@ -295,6 +356,7 @@
                 dot(hi_t[left, :], right_lo)
                 + dot(lo_t[left, :], right_hi)
                 + dot(hi_t[left, :], right_hi)
+                + ext[p, r]
             )
             for b in range(2):
                 q = 2 * p + b
@@ -335,12 +397,21 @@
 
     @pl.when((j == 1) & (z < 3))
     def _():
-        for cp in halo_copies:
+        for cp in ups:
             cp.wait_send()
 
+    @pl.when((j == 0) & (z > 0))
+    def _():
+        for cp in downs:
+            cp.wait_send()
+
     @pl.when(z > 0)
     def _():
-        forward.wait_send()
+        forwards[0].wait_send()
+
+    @pl.when(z < 3)
+    def _():
+        forwards[1].wait_send()
 
     for q in range(NQ):
         for copies in (*first_hop[q], second_hop[q], *z_hops[q]):
@@ -358,12 +429,18 @@
         kernel,
         out_shape=jax.ShapeDtypeStruct((width // 32, width), f32),
         in_specs=[
-            pl.BlockSpec(memory_space=pltpu.SMEM),
-            pl.BlockSpec(memory_space=pltpu.VMEM),
+            pl.BlockSpec(memory_space=pltpu.HBM),
+            pl.BlockSpec(memory_space=pltpu.HBM),
         ],
         out_specs=pl.BlockSpec(memory_space=pltpu.VMEM),
         scratch_shapes=[
+            pltpu.SMEM(lengths.shape, jnp.int32),
             pltpu.VMEM((3 * steps, width), bf16),
+            pltpu.VMEM((NQ // 2, 4, rows, 2 * cols), f32),
+            pltpu.VMEM((steps // 2, width), bf16),
+            pltpu.VMEM((steps // 2, width), bf16),
+            pltpu.VMEM((width, steps // 2), bf16),
+            pltpu.VMEM((width, steps // 2), bf16),
             pltpu.VMEM((8, 1, width), f32),
             pltpu.VMEM((2 * steps, width), bf16),
             pltpu.VMEM((2 * steps, width), bf16),
@@ -385,17 +462,18 @@
             pltpu.VMEM((NQ, 3, 2, cols), f32),
             pltpu.VMEM((NQ, rows // 4, cols), f32),
             pltpu.VMEM((NQ, rows // 8, cols), f32),
+            dma((2,)),
             dma((8,)), dma((8,)),
             dma, dma,
-            dma((2,)), dma,
-            dma, dma,
+            dma((2,)), dma((2,)),
+            dma((2,)), dma((2,)),
             dma((NQ, 2)), dma((NQ, 2)), dma((NQ, 2)), dma((NQ, 2)),
             dma((NQ,)), dma((NQ,)), dma((NQ,)), dma((NQ,)),
             dma((NQ, 3)), dma((NQ, 3)), dma((NQ, 3)), dma((NQ, 3)),
             dma((NQ,)), dma((NQ,)),
         ],
         compiler_params=pltpu.CompilerParams(
-            collective_id=0, has_side_effects=True, vmem_limit_bytes=48 * 1024 * 1024
+            collective_id=0, has_side_effects=True, vmem_limit_bytes=67043328
         ),
     )(lengths, traces.reshape(steps, width))
 

time: 36.8 us -> 33.6 us (0.913)
  Pallas kernels: 34.3 us -> 31.9 us
  local copies, waits for them, and re-layouts: 2.35 us -> 1.57 us
    pallas_call x1, Pallas kernels: 34.3 us -> 31.9 us  [fused(): pl.pallas_call(kernel, out_shape=jax.ShapeDtypeStruct((width // 32, width...]
    unnamed x5 -> x1, local copies, waits for them, and re-layouts: 2.35 us -> 1.57 us
where the time goes in v3:
time: 33.6 us; the launch traced here: 33.5 us
  Pallas kernels  31.9 us (95%)
  local copies, waits for them, and re-layouts  1.57 us (5%)
    pallas_call x1, Pallas kernels, fused(): pl.pallas_call(kernel, out_shape=jax.ShapeDtypeStruct((width // 32, width...  31.9 us
    unnamed x1, local copies, waits for them, and re-layouts  1.57 us

profile of v3, /device:TPU:0, one launch (start us, length us, event | category | flops | bytes accessed | tf_op | source)
XLA Modules:
  0.0 33.5 jit_solution(1076639020347654508)
XLA Ops:
  0.0 31.9 %shard_map.28 = f32[32,1024]{1,0:T(8,128)} custom-call(s32[4]{0:T(128)} %len_hbm.1, bf16[256,1024]{1,0:T(8,128)(2,1)} %bitcast.1), custom_call_target="tpu_custom_call" | custom-call | tf_op jit(solution)/shard_map/pallas_call | solution.py:428
  31.9 1.6 %copy.4 = f32[32,1024]{1,0:T(8,128)} copy(f32[32,1024]{1,0:T(8,128)} %shard_map.28) | data formatting | bytes 262144

commit v4 on v3

--- a/solution.py
+++ b/solution.py
@@ -75,17 +75,16 @@
 
 def kernel(
     len_hbm, x_hbm, o_ref, len_ref, data, ext, hi_e, lo_e, hi_et, lo_et, sums, hi, lo, hi_t, lo_t, keep, code1, scale1, got1,
-    gots1, code2, scale2, got2, gots2, plane, code3, scale3, got3, gots3, done, other, in_sem, s_sum, r_sum, s_x, r_x,
+    gots1, code2, scale2, got2, gots2, plane, code3, scale3, got3, gots3, in_sem, s_sum, r_sum, s_x, r_x,
     s_halo, r_halo, s_fwd, r_fwd, s1, r1, s1s,
-    r1s, s2, r2, s2s, r2s, s3, r3, s3s, r3s, s4, r4,
+    r1s, s2, r2, s2s, r2s, s3, r3, s3s, r3s,
 ):
     steps, width = x_hbm.shape
     pad = steps // 2
     half = width // 2
     cols = half // NQ
     rows = width // 4
-    zrows = rows // 4
-    orows = zrows // 2
+    orows = rows // 8
     c = lax.axis_index("chain")
     k = lax.axis_index("tm")
     z = k // 2
@@ -264,21 +263,24 @@
             copy(scales, to_scales, ss.at[at], rs.at[at], **where),
         ]
 
-    def pack(values, codes, scales, at):
+    def pack(values, codes, scales, at, flat=False):
         for g in range(8):
             v = values(g)
             top = jnp.maximum(jnp.max(jnp.abs(v), axis=0, keepdims=True), 1e-33)
-            scales[(*at, g // 2, slice(g % 2, g % 2 + 1))] = top * (1.0 / TOP)
+            place = (g,) if flat else (g // 2, slice(g % 2, g % 2 + 1))
+            scales[(*at, *place)] = top * (1.0 / TOP)
             code = jnp.round(v * (TOP / top)).astype(jnp.int32).astype(jnp.int16)
             codes[(*at, slice(32 * g, 32 * g + 32))] = code
 
-    def unpack(codes, scales, at, g, base=None):
+    def unpack(codes, scales, at, g):
         code = codes[(*at, slice(32 * g, 32 * g + 32))].astype(jnp.int32).astype(jnp.float32)
-        if base is None:
-            return code * scales[(*at, g // 2, slice(g % 2, g % 2 + 1))]
-        return code * scales[(*at, slice(g, g + 1))]
-
-    first_hop, second_hop, z_hops, swaps = [], [], [], []
+        return code * scales[(*at, g // 2, slice(g % 2, g % 2 + 1))]
+
+    first_hop, second_hop, z_hops = [], [], []
+
+    def goal(i):
+        return k ^ i
+
     for q in range(NQ):
         m1 = 1 + q % 2
         m2 = 3 - m1
@@ -297,18 +299,12 @@
         )
         z_hops.append([
             send(
-                code3.at[q, pl.ds(pl.multiple_of(zrows * (z ^ s), zrows), zrows), :],
-                scale3.at[q, z ^ s], got3.at[q, s - 1], gots3.at[q, s - 1],
-                ((s3, r3), (s3s, r3s)), (q, s - 1), tm=k ^ (2 * s),
+                code3.at[q, pl.ds(pl.multiple_of(goal(i) * orows, orows), orows), :],
+                scale3.at[q, goal(i)], got3.at[q, i - 1], gots3.at[q, i - 1],
+                ((s3, r3), (s3s, r3s)), (q, i - 1), tm=k ^ i,
             )
-            for s in range(1, 4)
+            for i in range(1, 8)
         ])
-        swaps.append(
-            copy(
-                done.at[q, pl.ds(pl.multiple_of(orows * (1 - j), orows), orows), :],
-                other.at[q], s4.at[q], r4.at[q], tm=k ^ 1,
-            )
-        )
 
     def hop2(q):
         arrive(first_hop[q][1])
@@ -331,20 +327,22 @@
             plane[q, 32 * g : 32 * g + 32] = v
             return v
 
-        pack(value, code3, scale3, (q,))
+        pack(value, code3, scale3, (q,), True)
         for copies in z_hops[q]:
             start(copies)
 
     def hop4(q):
-        for s in range(3):
-            arrive(z_hops[q][s])
-        for g in range(2):
-            at = pl.ds(pl.multiple_of(zrows * z + orows * g, orows), orows)
-            here = plane[q, at, :]
-            for s in range(3):
-                here = here + unpack(got3, gots3, (q, s), g, 0)
-            done[q, 32 * g : 32 * g + 32] = here * scale
-        swaps[q].start()
+        here = plane[q, pl.ds(pl.multiple_of(orows * k, orows), orows), :]
+        there = None
+        for i in (2, 4, 6, 1, 3, 5, 7):
+            arrive(z_hops[q][i - 1])
+            v = got3[q, i - 1].astype(jnp.int32).astype(jnp.float32) * gots3[q, i - 1]
+            if i % 2 == 0:
+                here = here + v
+            else:
+                there = v if there is None else there + v
+        o_ref[:, pl.ds(pl.multiple_of(half * j + cols * q, cols), cols)] = here * scale
+        o_ref[:, pl.ds(pl.multiple_of(half * (1 - j) + cols * q, cols), cols)] = there * scale
 
     def products(p, go):
         at = pl.ds(pl.multiple_of(half * j + 2 * cols * p, 2 * cols), 2 * cols)
@@ -384,13 +382,6 @@
     hop3(3)
     for q in range(NQ):
         hop4(q)
-    for q in range(NQ):
-        o_ref[:, pl.ds(pl.multiple_of(half * j + cols * q, cols), cols)] = done[
-            q, pl.ds(pl.multiple_of(orows * j, orows), orows), :
-        ]
-        swaps[q].wait_recv()
-        o_ref[:, pl.ds(pl.multiple_of(half * (1 - j) + cols * q, cols), cols)] = other[q]
-
     for cp in sum_copies:
         cp.wait_send()
     x_copy.wait_send()
@@ -417,7 +408,6 @@
         for copies in (*first_hop[q], second_hop[q], *z_hops[q]):
             for cp in copies:
                 cp.wait_send()
-        swaps[q].wait_send()
 
 
 def fused(traces, lengths):
@@ -457,11 +447,9 @@
             pltpu.VMEM((NQ, 4, 2, cols), f32),
             pltpu.VMEM((NQ, rows, cols), f32),
             pltpu.VMEM((NQ, rows, cols), i16),
-            pltpu.VMEM((NQ, 4, 2, cols), f32),
-            pltpu.VMEM((NQ, 3, rows // 4, cols), i16),
-            pltpu.VMEM((NQ, 3, 2, cols), f32),
-            pltpu.VMEM((NQ, rows // 4, cols), f32),
-            pltpu.VMEM((NQ, rows // 8, cols), f32),
+            pltpu.VMEM((NQ, 8, 1, cols), f32),
+            pltpu.VMEM((NQ, 7, rows // 8, cols), i16),
+            pltpu.VMEM((NQ, 7, 1, cols), f32),
             dma((2,)),
             dma((8,)), dma((8,)),
             dma, dma,
@@ -469,8 +457,7 @@
             dma((2,)), dma((2,)),
             dma((NQ, 2)), dma((NQ, 2)), dma((NQ, 2)), dma((NQ, 2)),
             dma((NQ,)), dma((NQ,)), dma((NQ,)), dma((NQ,)),
-            dma((NQ, 3)), dma((NQ, 3)), dma((NQ, 3)), dma((NQ, 3)),
-            dma((NQ,)), dma((NQ,)),
+            dma((NQ, 7)), dma((NQ, 7)), dma((NQ, 7)), dma((NQ, 7)),
         ],
         compiler_params=pltpu.CompilerParams(
             collective_id=0, has_side_effects=True, vmem_limit_bytes=67043328

time: 33.6 us -> 33.4 us (level)
  no operation moved by 1% of the time
where the time goes in v4:
time: 33.4 us; the launch traced here: 33.2 us
  Pallas kernels  31.7 us (95%)
  local copies, waits for them, and re-layouts  1.57 us (5%)
    pallas_call x1, Pallas kernels, fused(): pl.pallas_call(kernel, out_shape=jax.ShapeDtypeStruct((width // 32, width...  31.7 us
    unnamed x1, local copies, waits for them, and re-layouts  1.57 us

profile of v4, /device:TPU:0, one launch (start us, length us, event | category | flops | bytes accessed | tf_op | source)
XLA Modules:
  0.0 33.2 jit_solution(6370416611626885196)
XLA Ops:
  0.0 31.7 %shard_map.28 = f32[32,1024]{1,0:T(8,128)} custom-call(s32[4]{0:T(128)} %len_hbm.1, bf16[256,1024]{1,0:T(8,128)(2,1)} %bitcast.1), custom_call_target="tpu_custom_call" | custom-call | tf_op jit(solution)/shard_map/pallas_call | solution.py:418
  31.7 1.6 %copy.4 = f32[32,1024]{1,0:T(8,128)} copy(f32[32,1024]{1,0:T(8,128)} %shard_map.28) | data formatting | bytes 262144
